TPU v7x, 128 devices: a whole 4x4x4 slice. The times are simulated.
128 devices in a mesh: layer: 8 (over z, y_lo), blk: 16 (over x, y_hi, core).
Axes of the slice: x: 4, y: 4 (y_hi: 2, y_lo: 2; y = y_hi * 2 + y_lo), z: 4, core: 2. Of those that a mesh axis runs over, the one named last changes fastest.
Arguments:
- iterate: bfloat16 [8, 1536, 12288], P('layer', 'blk'), may hold values from -0.0546875 to 0.0546875
Outputs:
- update: bfloat16 [8, 1536, 12288], P(None, 'blk', 'layer')
All inputs are finite; a program needn't handle non-finite values.
Results may differ from a plain program's by a relative error of at most 0.0095.
Values may be sent and summed in bfloat16 or wider, within the bound.
No kernel may reach another device: no remote copies, remote signals or barrier semaphores. Data moves between devices by JAX's collectives and lax.ppermute only.
A program may use at most 128 MiB of HBM per device.

v0:
```python
import math
import jax
import jax.numpy as jnp
from jax import lax
from jax.sharding import PartitionSpec as P

coeff_a = 3.4445
coeff_b = -4.775
coeff_c = 2.0315


def shards(iterate):
    local_rows = iterate.shape[1]
    width = iterate.shape[2]
    all_rows = local_rows * lax.axis_size("blk")
    scale = math.sqrt(max(all_rows, width))
    pieces = lax.all_gather(iterate, "blk", axis=1, tiled=True)
    gathered = pieces
    gram_tile = jnp.einsum("lrc,lkc->lrk", iterate, pieces, preferred_element_type=jnp.float32)
    gram_block = gram_tile
    gathered, gram_block = (gathered, gram_block)
    gram_half = gram_block.astype(jnp.bfloat16)
    square = jnp.einsum(
        "lrk,lkm->lrm",
        gram_half,
        lax.all_gather(gram_half, "blk", axis=1, tiled=True),
        preferred_element_type=jnp.float32,
    )
    mixing = (coeff_b * gram_half.astype(jnp.float32) + coeff_c * square).astype(jnp.bfloat16)
    result = coeff_a * iterate.astype(jnp.float32) + jnp.einsum(
        "lrk,lkc->lrc", mixing, gathered, preferred_element_type=jnp.float32
    )
    scaled_rows = (scale * result).astype(jnp.bfloat16)
    return lax.all_to_all(scaled_rows, "layer", split_axis=2, concat_axis=0, tiled=True)


def solution(mesh):
    return jax.shard_map(
        shards,
        mesh=mesh,
        in_specs=(P("layer", "blk", None),),
        out_specs=P(None, "blk", "layer"),
        check_vma=False,
    )
```

profile of v0, /device:TPU:0, one launch (start us, length us, event | category | flops | bytes accessed | tf_op | source)
XLA Modules:
  0.0 465.5 jit_solution(16663097031767835544)
XLA Ops:
  6.5 0.0 all-gather.4.cloned.1.call-start
  6.5 0.7 all-gather.4.cloned.1.call-update
  7.3 0.0 copy-start
  7.3 0.0 all-gather.6.cloned.1.call-start
  7.3 211.9 %all-gather.4.cloned.1.call-done = bf16[1,1536,12288]{2,1,0:T(8,128)(2,1)} async-done(((bf16[1,96,12288]{2,1,0:T(8,128)(2,1)}), bf16[1,1536,12288]{2,1,0:T(8,128)(2,1)}) %all-gather.4.cloned.1.call-update) | async-done | bytes 37748752 | tf_op jit(solution)/shard_map/all_gather | solution.py:17
  219.2 18.5 %fusion.19 = bf16[96,1536]{1,0:T(8,128)(2,1)} fusion(bf16[1,1536,12288]{2,1,0:T(8,128)(2,1)} %all-gather.4.cloned.1.call-done, bf16[1,96,12288]{2,1,0:T(8,128)(2,1)} %param.1), kind=kOutput, calls=%fused_computation.13 | convolution fusion | flops 3624026112 | bytes 40402944 | tf_op jit(solution)/shard_map/lrc,lkc->lrk/dot_general | solution.py:19
  237.7 0.0 all-gather.6.cloned.1.call-update
  237.8 55.6 %all-gather.6.cloned.1.call-done = bf16[1536,1536]{1,0:T(8,128)(2,1)} async-done(((bf16[96,1536]{1,0:T(8,128)(2,1)}), bf16[1536,1536]{1,0:T(8,128)(2,1)}) %all-gather.6.cloned.1.call-update) | async-done | bytes 4718608 | tf_op jit(solution)/shard_map/all_gather | solution.py:26
  293.3 0.0 copy-done
  293.3 22.3 %fusion.13 = bf16[1,96,12288]{2,1,0:T(8,128)(2,1)} fusion(bf16[1,1536,12288]{2,1,0:T(8,128)(2,1)} %all-gather.4.cloned.1.call-done, bf16[1,96,12288]{2,1,0:T(8,128)(2,1)S(1)} %copy-done, bf16[96,1536]{1,0:T(8,128)(2,1)} %fusion.19, bf16[1536,1536]{1,0:T(8,128)(2,1)} %all-gather.6.cloned.1.call-done), kind=kOutput, calls=%fused_computation.7 | convolution fusion | flops 4083499008 | bytes 47480832 | tf_op jit(solution)/shard_map/lrk,lkc->lrc/dot_general | solution.py:30
  315.6 13.5 %copy.5 = bf16[1,96,12288]{1,0,2:T(2,128)(2,1)} copy(bf16[1,96,12288]{2,1,0:T(8,128)(2,1)} %fusion.13) | data formatting | bytes 4718592 | tf_op jit(solution)/shard_map/convert_element_type | solution.py:33
  329.1 0.5 broadcast.2
  329.7 67.2 %reduce = bf16[12288,96]{1,0:T(8,128)(2,1)S(1)} reduce(bf16[12288,1,96]{2,1,0:T(2,128)(2,1)} %bitcast.42, bf16[]{:T(256)} %broadcast.2), dimensions={1}, to_apply=%bitcast.37.reduce_sub_computation | reduce | bytes 4718594
  396.8 6.0 %reshape.28 = bf16[8,2,73728]{2,1,0:T(2,128)(2,1)} reshape(bf16[12288,96]{1,0:T(8,128)(2,1)S(1)} %reduce) | data formatting | bytes 4718592
  402.8 34.6 %all_to_all.18 = bf16[8,2,73728]{2,1,0:T(2,128)(2,1)S(1)} all-to-all(bf16[8,2,73728]{2,1,0:T(2,128)(2,1)} %reshape.28), channel_id=1, replica_groups=mesh['layer'=8,'blk'=16] {'layer'}, dimensions={0} | all-to-all | bytes 4718592 | tf_op jit(solution)/shard_map/all_to_all | solution.py:34
  437.4 6.1 %reshape.29 = bf16[12288,1,96]{2,1,0:T(2,128)(2,1)} reshape(bf16[8,2,73728]{2,1,0:T(2,128)(2,1)S(1)} %all_to_all.18) | data formatting | bytes 4718592
  443.5 12.1 %copy.6 = bf16[1,96,12288]{2,1,0:T(8,128)(2,1)S(1)} copy(bf16[1,96,12288]{1,0,2:T(2,128)(2,1)} %bitcast.43) | data formatting | bytes 4718592 | tf_op jit(solution)/shard_map/all_to_all | solution.py:34
  455.6 0.8 copy.8
  456.4 0.2 bitcast_bitcast_fusion
  456.5 2.1 copy.7
Async XLA Ops:
  6.5 212.7 %all-gather.4.cloned.1.call-start = ((), (), s32[]{:S(2)}) async-start(), calls=%async_computation.1 | async-start | bytes 40108032 | tf_op jit(solution)/shard_map/all_gather | solution.py:17
  7.3 286.1 %copy-start = (bf16[1,96,12288]{2,1,0:T(8,128)(2,1)S(1)}, bf16[1,96,12288]{2,1,0:T(8,128)(2,1)}, u32[]{:S(2)}) copy-start(bf16[1,96,12288]{2,1,0:T(8,128)(2,1)} %param.1) | copy-start | bytes 7077892
  7.3 286.1 %all-gather.6.cloned.1.call-start = ((), (), s32[]{:S(2)}) async-start(), calls=%async_computation.2 | async-start | bytes 5013504 | tf_op jit(solution)/shard_map/all_gather | solution.py:26
Sparse Core Ops, SparseCore 0:
  9.8 209.4 all-gather.3
  237.9 55.3 all-gather.5
where the time goes:
time: 466 us; the launch traced here: 465 us
  waiting for transfers between devices  268 us (58%)
  other arithmetic  67.2 us (14%)
  local copies, waits for them, and re-layouts  41.2 us (9%)
  matrix products  40.8 us (9%)
  blocking collectives  34.6 us (7%)
  between operations  13.4 us (3%)
    all_gather x1, waiting for transfers between devices, shards(): pieces = lax.all_gather(iterate, 'blk', axis=1, tiled=True)  212 us
    unnamed x1, other arithmetic  67.2 us
    all_gather x1, waiting for transfers between devices, shards(): lax.all_gather(gram_half, 'blk', axis=1, tiled=True)  55.6 us
    all_to_all x1, blocking collectives, shards(): lax.all_to_all(scaled_rows, 'layer', split_axis=2, concat_axis=0, tiled=T...  34.6 us
    dot_general x1, matrix products, shards(): jnp.einsum('lrk,lkc->lrc', mixing, gathered, preferred_element_type=jnp.f...  22.3 us
    dot_general x1, matrix products, shards(): jnp.einsum('lrc,lkc->lrk', iterate, pieces, preferred_element_type=jnp.fl...  18.5 us
    all_to_all x3, local copies, waits for them, and re-layouts, shards(): lax.all_to_all(scaled_rows, 'layer', split_axis=2, concat_axis=0, tiled=T...  14.3 us
    convert_element_type x1, local copies, waits for them, and re-layouts, shards(): scaled_rows = (scale * result).astype(jnp.bfloat16)  13.5 us
  transfers between devices with their start and end apart: 2, of which 2 were waited for; matrix products, arithmetic and copies ran while one was open for 0% of the time, Pallas kernels for 0%

commit v1 on v0

--- a/solution.py
+++ b/solution.py
@@ -31,7 +31,12 @@
         "lrk,lkc->lrc", mixing, gathered, preferred_element_type=jnp.float32
     )
     scaled_rows = (scale * result).astype(jnp.bfloat16)
-    return lax.all_to_all(scaled_rows, "layer", split_axis=2, concat_axis=0, tiled=True)
+    return jnp.concatenate(
+        lax.all_to_all(
+            jnp.stack(jnp.split(scaled_rows, lax.axis_size("layer"), axis=2)), "layer", 0, 0
+        ),
+        axis=0,
+    )
 
 
 def solution(mesh):

time: 466 us -> 366 us (0.79)
  other arithmetic: 67.2 us -> 0 us
  local copies, waits for them, and re-layouts: 41.2 us -> 9.28 us
    unnamed x1 -> x0, other arithmetic: 67.2 us -> none
    all_to_all x3 -> x0, local copies, waits for them, and re-layouts: 14.3 us -> none  [shards(): lax.all_to_all(scaled_rows, 'layer', split_axis=2, concat_axis=0, tiled=T...]
    convert_element_type x1 -> x0, local copies, waits for them, and re-layouts: 13.5 us -> none  [shards(): scaled_rows = (scale * result).astype(jnp.bfloat16)]
    unnamed x6 -> x10, local copies, waits for them, and re-layouts: 13.4 us -> 8.3 us
where the time goes in v1:
time: 366 us
  waiting for transfers between devices  268 us (73%)
  matrix products  40.2 us (11%)
  blocking collectives  34.4 us (9%)
  between operations  13.4 us (4%)
  local copies, waits for them, and re-layouts  9.28 us (3%)
    all_gather x1, waiting for transfers between devices, shards(): pieces = lax.all_gather(iterate, 'blk', axis=1, tiled=True)  212 us
    all_gather x1, waiting for transfers between devices, shards(): lax.all_gather(gram_half, 'blk', axis=1, tiled=True)  55.6 us
    all_to_all x1, blocking collectives, shards(): lax.all_to_all(jnp.stack(jnp.split(scaled_rows, lax.axis_size('layer'), a...  34.4 us
    dot_general x1, matrix products, shards(): jnp.einsum('lrk,lkc->lrc', mixing, gathered, preferred_element_type=jnp.f...  22.3 us
    dot_general x1, matrix products, shards(): jnp.einsum('lrc,lkc->lrk', iterate, pieces, preferred_element_type=jnp.fl...  17.8 us
    unnamed x10, local copies, waits for them, and re-layouts  8.3 us
  transfers between devices with their start and end apart: 2, of which 2 were waited for; matrix products, arithmetic and copies ran while one was open for 0% of the time, Pallas kernels for 0%

profile of v1, /device:TPU:0, one launch (start us, length us, event | category | flops | bytes accessed | tf_op | source)
XLA Modules:
  0.0 365.6 jit_solution(12927268568163251979)
XLA Ops:
  6.5 0.0 copy-start
  6.5 0.0 all-gather.4.cloned.1.call-start
  6.5 0.7 all-gather.4.cloned.1.call-update
  7.3 0.0 all-gather.6.cloned.1.call-start
  7.3 211.9 %all-gather.4.cloned.1.call-done = bf16[1,1536,12288]{2,1,0:T(8,128)(2,1)} async-done(((bf16[1,96,12288]{2,1,0:T(8,128)(2,1)}), bf16[1,1536,12288]{2,1,0:T(8,128)(2,1)}) %all-gather.4.cloned.1.call-update) | async-done | bytes 37748752 | tf_op jit(solution)/shard_map/all_gather | solution.py:17
  219.2 0.0 copy-done
  219.2 17.8 %fusion.19 = bf16[96,1536]{1,0:T(8,128)(2,1)} fusion(bf16[1,1536,12288]{2,1,0:T(8,128)(2,1)} %all-gather.4.cloned.1.call-done, bf16[1,96,12288]{2,1,0:T(8,128)(2,1)S(1)} %copy-done), kind=kOutput, calls=%fused_computation.12 | convolution fusion | flops 3624026112 | bytes 40402944 | tf_op jit(solution)/shard_map/lrc,lkc->lrk/dot_general | solution.py:19
  237.1 0.0 all-gather.6.cloned.1.call-update
  237.1 55.6 %all-gather.6.cloned.1.call-done = bf16[1536,1536]{1,0:T(8,128)(2,1)} async-done(((bf16[96,1536]{1,0:T(8,128)(2,1)}), bf16[1536,1536]{1,0:T(8,128)(2,1)}) %all-gather.6.cloned.1.call-update) | async-done | bytes 4718608 | tf_op jit(solution)/shard_map/all_gather | solution.py:26
  292.7 22.3 %fusion.13 = bf16[1,96,12288]{2,1,0:T(8,128)(2,1)} fusion(bf16[1,1536,12288]{2,1,0:T(8,128)(2,1)} %all-gather.4.cloned.1.call-done, bf16[1,96,12288]{2,1,0:T(8,128)(2,1)S(1)} %copy-done, bf16[96,1536]{1,0:T(8,128)(2,1)} %fusion.19, bf16[1536,1536]{1,0:T(8,128)(2,1)} %all-gather.6.cloned.1.call-done), kind=kOutput, calls=%fused_computation.7 | convolution fusion | flops 4083499008 | bytes 47480832 | tf_op jit(solution)/shard_map/lrk,lkc->lrc/dot_general | solution.py:30
  315.0 1.0 fusion.33
  316.0 1.0 fusion.32
  317.0 1.0 fusion.31
  318.0 1.0 fusion.30
  319.0 1.0 fusion.29
  319.9 1.0 fusion.28
  320.9 1.0 fusion.27
  321.9 1.0 fusion.26
  322.9 34.4 %all_to_all.5 = bf16[8,1,96,1536]{3,2,1,0:T(8,128)(2,1)S(1)} all-to-all(bf16[8,1,96,1536]{3,2,1,0:T(8,128)(2,1)S(1)} %fusion.26), channel_id=1, replica_groups=mesh['layer'=8,'blk'=16] {'layer'}, dimensions={0} | all-to-all | bytes 4718592 | tf_op jit(solution)/shard_map/all_to_all | solution.py:35
  357.3 1.4 copy.10
Async XLA Ops:
  6.5 212.7 %copy-start = (bf16[1,96,12288]{2,1,0:T(8,128)(2,1)S(1)}, bf16[1,96,12288]{2,1,0:T(8,128)(2,1)}, u32[]{:S(2)}) copy-start(bf16[1,96,12288]{2,1,0:T(8,128)(2,1)} %param.1) | copy-start | bytes 7077892
  6.5 212.7 %all-gather.4.cloned.1.call-start = ((), (), s32[]{:S(2)}) async-start(), calls=%async_computation.1 | async-start | bytes 40108032 | tf_op jit(solution)/shard_map/all_gather | solution.py:17
  7.3 285.4 %all-gather.6.cloned.1.call-start = ((), (), s32[]{:S(2)}) async-start(), calls=%async_computation.2 | async-start | bytes 5013504 | tf_op jit(solution)/shard_map/all_gather | solution.py:26
Sparse Core Ops, SparseCore 0:
  9.8 209.4 all-gather.3
  237.2 55.3 all-gather.5

commit v2 on v0

--- a/solution.py
+++ b/solution.py
@@ -14,7 +14,9 @@
     width = iterate.shape[2]
     all_rows = local_rows * lax.axis_size("blk")
     scale = math.sqrt(max(all_rows, width))
-    pieces = lax.all_gather(iterate, "blk", axis=1, tiled=True)
+    pieces = jnp.concatenate(
+        lax.all_to_all(jnp.stack([iterate] * lax.axis_size("blk")), "blk", 0, 0), axis=1
+    )
     gathered = pieces
     gram_tile = jnp.einsum("lrc,lkc->lrk", iterate, pieces, preferred_element_type=jnp.float32)
     gram_block = gram_tile

time: 466 us -> 687 us (1.47)
  blocking collectives: 34.6 us -> 454 us
  waiting for transfers between devices: 268 us -> 56.8 us
  local copies, waits for them, and re-layouts: 41.2 us -> 54.8 us
    all_to_all x0 -> x1, blocking collectives: none -> 420 us  [shards(): lax.all_to_all(jnp.stack([iterate] * lax.axis_size('blk')), 'blk', 0, 0)]
    all_gather x1 -> x0, waiting for transfers between devices: 212 us -> none  [shards(): pieces = lax.all_gather(iterate, 'blk', axis=1, tiled=True)]
    another operation x0 -> x1, local copies, waits for them, and re-layouts: none -> 13.6 us  [shards(): jnp.stack([iterate] * lax.axis_size('blk'))]
  transfers between devices with their start and end apart: 2 -> 1, of which waited for: 2 -> 1; matrix products, arithmetic and copies ran while one was open for 0% -> 0% of each run, Pallas kernels for 0% -> 0%
where the time goes in v2:
time: 687 us; the launch traced here: 686 us
  blocking collectives  454 us (66%)
  other arithmetic  67.2 us (10%)
  waiting for transfers between devices  56.8 us (8%)
  local copies, waits for them, and re-layouts  54.8 us (8%)
  matrix products  40.1 us (6%)
  between operations  13.4 us (2%)
    all_to_all x1, blocking collectives, shards(): lax.all_to_all(jnp.stack([iterate] * lax.axis_size('blk')), 'blk', 0, 0)  420 us
    unnamed x1, other arithmetic  67.2 us
    all_gather x1, waiting for transfers between devices, shards(): lax.all_gather(gram_half, 'blk', axis=1, tiled=True)  56.8 us
    all_to_all x1, blocking collectives, shards(): lax.all_to_all(scaled_rows, 'layer', split_axis=2, concat_axis=0, tiled=T...  34.6 us
    dot_general x1, matrix products, shards(): jnp.einsum('lrk,lkc->lrc', mixing, gathered, preferred_element_type=jnp.f...  22.3 us
    dot_general x1, matrix products, shards(): jnp.einsum('lrc,lkc->lrk', iterate, pieces, preferred_element_type=jnp.fl...  17.8 us
    all_to_all x3, local copies, waits for them, and re-layouts, shards(): lax.all_to_all(scaled_rows, 'layer', split_axis=2, concat_axis=0, tiled=T...  14.3 us
  transfers between devices with their start and end apart: 1, of which 1 were waited for; matrix products, arithmetic and copies ran while one was open for 0% of the time, Pallas kernels for 0%

profile of v2, /device:TPU:0, one launch (start us, length us, event | category | flops | bytes accessed | tf_op | source)
XLA Modules:
  0.0 686.4 jit_solution(1221242351155050314)
XLA Ops:
  6.5 0.0 all-gather.3.cloned.1.call-start
  6.5 13.6 %stack.2 = bf16[16,1,96,12288]{3,2,1,0:T(8,128)(2,1)} broadcast(bf16[96,12288]{1,0:T(8,128)(2,1)} %bitcast.32), dimensions={2,3} | broadcast | bytes 40108032 | tf_op jit(solution)/shard_map/stack | solution.py:18
  20.1 0.0 copy-start
  20.1 419.6 %all_to_all.23 = bf16[16,1,96,12288]{3,2,1,0:T(8,128)(2,1)} all-to-all(bf16[16,1,96,12288]{3,2,1,0:T(8,128)(2,1)} %stack.2), channel_id=1, replica_groups=mesh['layer'=8,'blk'=16] {'blk'}, dimensions={0} | all-to-all | bytes 75497472 | tf_op jit(solution)/shard_map/all_to_all | solution.py:18
  439.7 0.0 copy-done
  439.7 17.8 %convolution_convert_fusion = bf16[96,1536]{1,0:T(8,128)(2,1)} fusion(bf16[1536,12288]{1,0:T(8,128)(2,1)} %bitcast.28, bf16[1,96,12288]{2,1,0:T(8,128)(2,1)S(1)} %copy-done), kind=kOutput, calls=%fused_computation.8 | convolution fusion | flops 3624026112 | bytes 40402944 | tf_op jit(solution)/shard_map/lrc,lkc->lrk/dot_general | solution.py:21
  457.5 0.0 all-gather.3.cloned.1.call-update
  457.5 56.8 %all-gather.3.cloned.1.call-done = bf16[1536,1536]{1,0:T(8,128)(2,1)} async-done(((bf16[96,1536]{1,0:T(8,128)(2,1)}), bf16[1536,1536]{1,0:T(8,128)(2,1)}) %all-gather.3.cloned.1.call-update) | async-done | bytes 4718608 | tf_op jit(solution)/shard_map/all_gather | solution.py:28
  514.3 22.3 %fusion.2 = bf16[1,96,12288]{2,1,0:T(8,128)(2,1)} fusion(bf16[1536,12288]{1,0:T(8,128)(2,1)} %bitcast.29, bf16[1,96,12288]{2,1,0:T(8,128)(2,1)S(1)} %copy-done, bf16[96,1536]{1,0:T(8,128)(2,1)} %convolution_convert_fusion, bf16[1536,1536]{1,0:T(8,128)(2,1)} %all-gather.3.cloned.1.call-done), kind=kOutput, calls=%fused_computation.3 | convolution fusion | flops 4083499008 | bytes 47480832 | tf_op jit(solution)/shard_map/lrk,lkc->lrc/dot_general | solution.py:32
  536.6 13.5 %copy.5 = bf16[1,96,12288]{1,0,2:T(2,128)(2,1)} copy(bf16[1,96,12288]{2,1,0:T(8,128)(2,1)} %fusion.2) | data formatting | bytes 4718592 | tf_op jit(solution)/shard_map/convert_element_type | solution.py:35
  550.1 0.5 broadcast.5
  550.6 67.2 %reduce = bf16[12288,96]{1,0:T(8,128)(2,1)S(1)} reduce(bf16[12288,1,96]{2,1,0:T(2,128)(2,1)} %bitcast.30, bf16[]{:T(256)} %broadcast.5), dimensions={1}, to_apply=%bitcast.21.reduce_sub_computation | reduce | bytes 4718594
  617.8 6.0 reshape.34
  623.8 34.6 %all_to_all.24 = bf16[8,2,73728]{2,1,0:T(2,128)(2,1)S(1)} all-to-all(bf16[8,2,73728]{2,1,0:T(2,128)(2,1)} %reshape.34), channel_id=1, replica_groups=mesh['layer'=8,'blk'=16] {'layer'}, dimensions={0} | all-to-all | bytes 4718592 | tf_op jit(solution)/shard_map/all_to_all | solution.py:36
  658.4 6.0 reshape.35
  664.5 12.1 %copy.6 = bf16[1,96,12288]{2,1,0:T(8,128)(2,1)S(1)} copy(bf16[1,96,12288]{1,0,2:T(2,128)(2,1)} %bitcast.31) | data formatting | bytes 4718592 | tf_op jit(solution)/shard_map/all_to_all | solution.py:36
  676.5 0.8 copy.8
  677.3 0.2 bitcast_bitcast_fusion
  677.5 2.1 copy.7
Async XLA Ops:
  6.5 507.8 %all-gather.3.cloned.1.call-start = ((), (), s32[]{:S(2)}) async-start(), calls=%async_computation.2 | async-start | bytes 5013504 | tf_op jit(solution)/shard_map/all_gather | solution.py:28
  20.1 419.6 %copy-start = (bf16[1,96,12288]{2,1,0:T(8,128)(2,1)S(1)}, bf16[1,96,12288]{2,1,0:T(8,128)(2,1)}, u32[]{:S(2)}) copy-start(bf16[1,96,12288]{2,1,0:T(8,128)(2,1)} %param.1) | copy-start | bytes 7077892
Sparse Core Ops, SparseCore 0:
  457.6 56.6 all-gather.2
